TPU v7x, 32 devices: a whole 2x2x4 slice. The times are simulated.
32 devices in a mesh: dp: 8 (over z, y), mp: 4 (over x, core).
Axes of the slice: x: 2, y: 2, z: 4, core: 2. Of those that a mesh axis runs over, the one named last changes fastest.
Arguments:
- embedded: bfloat16 [32, 64, 4096], P('dp', None, 'mp'), may hold values from -6 to 6
- targets: int32 [32, 64], P('dp'), may hold values from 0 to 65535
- labels: int32 [32], P('dp'), may hold values from 0 to 21
- counts: int32 [8], replicated, may hold values from 0 to 4, as said below
- destinations: int32 [32], P('dp'), may hold values from 0 to 15, as said below
- gain_in: float32 [4096], replicated, may hold values from 0.1 to 1.9
- w_query: bfloat16 [4096, 2048], P(None, 'mp'), may hold values from -40 to 40
- w_key: bfloat16 [4096, 1024], P(None, 'mp'), may hold values from -0.09375 to 0.09375
- w_value: bfloat16 [4096, 1024], P(None, 'mp'), may hold values from -0.09375 to 0.09375
- w_out: bfloat16 [2048, 4096], P('mp'), may hold values from -0.5 to 0.5
- gain_out: float32 [4096], replicated, may hold values from 0.1 to 1.9
- w_vocab: bfloat16 [4096, 65536], P('mp', 'dp'), may hold values from -40 to 40
- prev_probs: float32 [22], replicated, may hold values from 0.03 to 0.2
- log_weights: float32 [22], replicated, may hold values from -200 to 21000
Outputs:
- token_loss: float32 [1024], P(('dp', 'mp'))
- new_weights: float32 [22], replicated
- probs: float32 [22], replicated
Inputs may be any that keep to these rules, and one draw needn't show every extreme that they name: The counts sum to 16. `destinations`: each value from 0 to 15 is held by exactly one live slot; entries of slots that are not live are meaningless.
All inputs are finite; a program needn't handle non-finite values.
Results may differ from a plain program's by a relative error of at most 0.015.
The roundings to bfloat16 on the way count: a program that leaves them out, or rounds other values in their place, can miss the bound.
Values may be sent and summed in bfloat16 or wider, within the bound.
A program may use at most 192 MiB of HBM per device.

v0:
```python
import jax
import jax.numpy as jnp
from jax import lax
from jax.sharding import PartitionSpec as P

HEAD_DIM = 128
DOMAINS = 22
SEQ_DEV = 2
norm_eps = 1e-05
rope_base = 500000.0
memory_rate = 0.9
step_rate = 0.02
explore_mass = 0.005


def normalize(values, gain_vec):
    inv_rms = lax.rsqrt(jnp.mean(values * values, axis=-1, keepdims=True) + norm_eps)
    return values * inv_rms * gain_vec


def rotate_halves(tensor):
    full_width = tensor.shape[-1]
    half_width = full_width // 2
    frequency = jnp.power(
        jnp.float32(rope_base), -jnp.arange(half_width, dtype=jnp.float32) * 2.0 / full_width
    )
    angles = jnp.arange(tensor.shape[1], dtype=jnp.float32)[:, None] * frequency[None, :]
    cosine = jnp.cos(angles)[None, :, None, :]
    sine_part = jnp.sin(angles)[None, :, None, :]
    first_half = tensor[..., :half_width]
    second = tensor[..., half_width:]
    return jnp.concatenate(
        [first_half * cosine - second * sine_part, second * cosine + first_half * sine_part],
        axis=-1,
    )


def local(
    embedded,
    targets,
    labels,
    counts,
    destinations,
    gain_in,
    w_query,
    w_key,
    w_value,
    w_out,
    gain_out,
    w_vocab,
    prev_probs,
    log_weights,
):
    data_count = lax.axis_size("dp")
    data_index = lax.axis_index("dp")
    model_shard_count = lax.axis_size("mp")
    model_index = lax.axis_index("mp")
    slot_count = embedded.shape[0]
    seq_len = embedded.shape[1]
    seq_held = SEQ_DEV
    gathered_rows = (
        lax.all_gather(embedded, "dp", axis=0, tiled=True),
        lax.all_gather(targets, "dp", axis=0, tiled=True),
        lax.all_gather(labels, "dp", axis=0, tiled=True),
        lax.all_gather(destinations, "dp", axis=0, tiled=True),
    )
    slot_ids = jnp.arange(data_count * slot_count, dtype=jnp.int32)
    is_live = slot_ids % slot_count < counts[slot_ids // slot_count]
    wanted = data_index * seq_held + jnp.arange(seq_held, dtype=jnp.int32)
    picking_mask = (gathered_rows[3][None, :] == wanted[:, None]) & is_live[None, :]
    sequence_rows = jnp.einsum(
        "av,vyr->ayr",
        picking_mask.astype(jnp.bfloat16),
        gathered_rows[0],
        preferred_element_type=jnp.float32,
    ).astype(jnp.bfloat16)
    seq_targets = jnp.einsum("gs,sl->gl", picking_mask.astype(jnp.int32), gathered_rows[1])
    seq_labels = jnp.sum(jnp.where(picking_mask, gathered_rows[2][None, :], 0), axis=1).astype(
        jnp.int32
    )
    full_rows = lax.all_gather(sequence_rows, "mp", axis=2, tiled=True)
    rows_all = seq_held * seq_len
    flat_rows = full_rows.reshape(rows_all, -1).astype(jnp.float32)
    normed = normalize(flat_rows, gain_in).astype(jnp.bfloat16)
    local_heads = w_query.shape[1] // HEAD_DIM
    local_groups = w_key.shape[1] // HEAD_DIM
    query_heads = jnp.dot(normed, w_query, preferred_element_type=jnp.float32).reshape(
        seq_held, seq_len, local_heads, HEAD_DIM
    )
    key_heads = jnp.dot(normed, w_key, preferred_element_type=jnp.float32).reshape(
        seq_held, seq_len, local_groups, HEAD_DIM
    )
    value_heads = (
        jnp.dot(normed, w_value, preferred_element_type=jnp.float32)
        .astype(jnp.bfloat16)
        .reshape(seq_held, seq_len, local_groups, HEAD_DIM)
    )
    query_heads = rotate_halves(query_heads).astype(jnp.bfloat16)
    key_heads = rotate_halves(key_heads).astype(jnp.bfloat16)
    group_size = local_heads // local_groups
    key_heads = jnp.repeat(key_heads, group_size, axis=2)
    value_heads = jnp.repeat(value_heads, group_size, axis=2)
    scores = jnp.einsum(
        "sqhe,skhe->shqk", query_heads, key_heads, preferred_element_type=jnp.float32
    ) * HEAD_DIM ** (-0.5)
    causal = jnp.arange(seq_len)[:, None] >= jnp.arange(seq_len)[None, :]
    scores = jnp.where(causal[None, None], scores, -jnp.inf)
    weights = jax.nn.softmax(scores, axis=-1).astype(jnp.bfloat16)
    mixed_heads = jnp.einsum(
        "shqk,skhe->sqhe", weights, value_heads, preferred_element_type=jnp.float32
    )
    mixed_heads = mixed_heads.astype(jnp.bfloat16).reshape(rows_all, local_heads * HEAD_DIM)
    row_block_tiles = rows_all // model_shard_count
    update = lax.psum_scatter(
        jnp.dot(mixed_heads, w_out, preferred_element_type=jnp.float32).astype(jnp.bfloat16),
        "mp",
        scatter_dimension=0,
        tiled=True,
    ).astype(jnp.float32)
    my_start = model_index * row_block_tiles
    own_rows = lax.dynamic_slice_in_dim(flat_rows, my_start, row_block_tiles, 0)
    hidden = own_rows + update
    final_rows = normalize(hidden, gain_out).astype(jnp.bfloat16)
    own_targets = lax.dynamic_slice_in_dim(
        seq_targets.reshape(rows_all), my_start, row_block_tiles, 0
    )
    own_labels = lax.dynamic_slice_in_dim(
        jnp.repeat(seq_labels, seq_len), my_start, row_block_tiles, 0
    )
    everyone = (
        lax.all_gather(final_rows, "dp", axis=0, tiled=True),
        lax.all_gather(own_targets, "dp", axis=0, tiled=True),
        lax.all_gather(own_labels, "dp", axis=0, tiled=True),
    )
    all_rows = everyone[0]
    all_goals = everyone[1]
    all_kinds = everyone[2]
    vocab_local = w_vocab.shape[1]
    logits = jnp.dot(
        all_rows,
        lax.all_gather(w_vocab, "mp", axis=0, tiled=True),
        preferred_element_type=jnp.float32,
    )
    row_top = jnp.max(logits, axis=1)
    spread = jnp.sum(jnp.exp(logits - row_top[:, None]), axis=1)
    column_ids = all_goals - data_index * vocab_local
    picked = jnp.sum(
        jnp.where(
            jnp.arange(vocab_local, dtype=jnp.int32)[None, :] == column_ids[:, None], logits, 0.0
        ),
        axis=1,
    )
    top_all = lax.pmax(row_top, "dp")
    summed = lax.psum((spread * jnp.exp(row_top - top_all), picked), "dp")
    spread_all = summed[0]
    picked_all = summed[1]
    losses = top_all + jnp.log(spread_all) - picked_all
    own_loss = lax.dynamic_slice_in_dim(losses, data_index * row_block_tiles, row_block_tiles, 0)
    domains = jnp.arange(DOMAINS, dtype=jnp.int32)
    member = (all_kinds[:, None] == domains[None, :]).astype(jnp.float32)
    totals = lax.psum((jnp.sum(member * losses[:, None], axis=0), jnp.sum(member, axis=0)), "mp")
    loss_sums = totals[0]
    token_tally = totals[1]
    reward = loss_sums / jnp.maximum(token_tally, 1.0) / prev_probs
    new_weights = memory_rate * log_weights + (1.0 - memory_rate) * reward
    probs = (1.0 - DOMAINS * explore_mass) * jax.nn.softmax(step_rate * new_weights) + explore_mass
    return (own_loss, new_weights, probs)


def solution(mesh):
    placed = (
        P("dp", None, "mp"),
        P("dp", None),
        P("dp"),
        P(),
        P("dp"),
        P(),
        P(None, "mp"),
        P(None, "mp"),
        P(None, "mp"),
        P("mp", None),
        P(),
        P("mp", "dp"),
        P(),
        P(),
    )
    return jax.shard_map(
        local, mesh=mesh, in_specs=placed, out_specs=(P(("dp", "mp")), P(), P()), check_vma=False
    )
```

profile of v0, /device:TPU:0, one launch (start us, length us, event | category | flops | bytes accessed | tf_op | source)
XLA Modules:
  0.0 688.2 jit_solution(7423845925654693603)
XLA Ops:
  7.2 0.7 all-gather.6.cloned.1.call-update
  8.0 1.2 dynamic-slice
  9.9 0.9 dynamic-update-slice
  10.7 0.8 dynamic-update-slice.2
  11.6 1.4 gather_fusion
  13.0 13.6 %all-reduce.5 = (s32[32]{0:T(128)S(1)}, s32[32]{0:T(128)S(1)}) all-reduce(s32[32]{0:T(128)S(1)} %dynamic-update-slice, s32[32]{0:T(128)S(1)} %dynamic-update-slice.2), channel_id=1, replica_groups=mesh['dp'=8,'mp'=4] {'dp'}, use_global_device_ids=true, to_apply=%add | all-reduce | flops 64 | bytes 512
  26.5 0.7 select_reduce_fusion.2
  27.2 58.5 %all-gather.6.cloned.1.call-done = bf16[32,64,1024]{2,1,0:T(8,128)(2,1)} async-done(((bf16[4,64,1024]{2,1,0:T(8,128)(2,1)}), bf16[32,64,1024]{2,1,0:T(8,128)(2,1)}) %all-gather.6.cloned.1.call-update) | async-done | bytes 4194320 | tf_op jit(solution)/shard_map/all_gather | solution.py:62
  85.7 6.8 fusion.1
  92.5 0.8 copy.77
  93.3 4.1 copy.67
  97.5 6.5 copy.66
  104.0 0.1 fusion.21
  104.1 4.5 all-gather.8.cloned.1.call-done
  108.7 1.5 multiply_reduce_fusion
  110.3 2.8 fusion.10
  113.1 0.1 subtract_convert_fusion.1
  113.2 3.7 fusion.12
  117.0 0.2 subtract_convert_fusion
  117.2 0.9 fusion.34
  118.2 1.0 fusion.4
  119.2 0.3 bitcast_convert_fusion
  119.5 1.3 copy-done.1
  120.8 0.5 convolution_convert_fusion.2
  121.4 0.1 copy-done.11
  121.5 1.3 fusion.6
  122.9 3.9 convolution_convert_fusion
  126.9 24.9 %reduce-scatter.2.cloned.1.call-done = bf16[32,4096]{1,0:T(8,128)(2,1)} async-done(((bf16[128,4096]{1,0:T(8,128)(2,1)}), bf16[32,4096]{1,0:T(8,128)(2,1)}) %reduce-scatter.2.cloned.1.call-update) | async-done | bytes 262160 | tf_op jit(solution)/shard_map/reduce_scatter | solution.py:114
  151.8 1.3 multiply_reduce_fusion.1
  153.1 1.9 multiply_convert_fusion.3
  155.1 0.5 all-gather.12.cloned.1.call-update
  156.5 26.2 %all-gather = s32[8,4,64]{2,1,0:T(4,128)S(1)} all-gather(s32[1,4,64]{2,1,0:T(4,128)S(1)} %bitcast.56), channel_id=1, replica_groups=mesh['dp'=8,'mp'=4] {'dp'}, dimensions={0}, use_global_device_ids=true | all-gather | bytes 9216 | tf_op jit(solution)/shard_map/all_gather | solution.py:63
  182.7 0.1 fusion.38
  182.9 0.2 dynamic-slice_dynamic-update-slice_fusion
  183.1 0.2 dynamic-slice_dynamic-update-slice_fusion.1
  183.2 10.0 %all-reduce.4 = (s32[256]{0:T(256)S(1)}, s32[256]{0:T(256)S(1)}) all-reduce(s32[256]{0:T(256)S(1)} %dynamic-slice_dynamic-update-slice_fusion.1, s32[256]{0:T(256)S(1)} %dynamic-slice_dynamic-update-slice_fusion), channel_id=1, replica_groups=mesh['dp'=8,'mp'=4] {'dp'}, use_global_device_ids=true, to_apply=%add.1 | all-reduce | flops 512 | bytes 4096
  193.3 11.1 %all-gather.10.cloned.1.call-done = bf16[256,4096]{1,0:T(8,128)(2,1)} async-done(((bf16[32,4096]{1,0:T(8,128)(2,1)}), bf16[256,4096]{1,0:T(8,128)(2,1)}) %all-gather.10.cloned.1.call-update) | async-done | bytes 2097168 | tf_op jit(solution)/shard_map/all_gather | solution.py:131
  204.4 392.7 %all-gather.12.cloned.1.call-done = bf16[4096,8192]{1,0:T(8,128)(2,1)} async-done(((bf16[1024,8192]{1,0:T(8,128)(2,1)}), bf16[4096,8192]{1,0:T(8,128)(2,1)}) %all-gather.12.cloned.1.call-update) | async-done | bytes 67108880 | tf_op jit(solution)/shard_map/all_gather | solution.py:141
  597.1 30.6 %fusion.37 = (f32[256]{0:T(256)S(1)}, f32[256,8192]{1,0:T(8,128)}) fusion(bf16[256,4096]{1,0:T(8,128)(2,1)} %all-gather.10.cloned.1.call-done, bf16[4096,8192]{1,0:T(8,128)(2,1)} %all-gather.12.cloned.1.call-done), kind=kOutput, calls=%fused_computation.79 | convolution fusion | flops 17181966336 | bytes 77595648 | tf_op jit(solution)/shard_map/dot_general | solution.py:139
  627.7 21.3 %pmax.7 = f32[256]{0:T(256)S(1)} all-reduce(f32[256]{0:T(256)S(1)} %get-tuple-element.25), channel_id=1, replica_groups=mesh['dp'=8,'mp'=4] {'dp'}, use_global_device_ids=true, to_apply=%region_6.7 | all-reduce | flops 256 | bytes 2048 | tf_op jit(solution)/shard_map/pmax | solution.py:153
  649.0 5.1 exponential_reduce_fusion
  654.1 17.1 %all-reduce.6 = (f32[256]{0:T(256)S(1)}, f32[256]{0:T(256)S(1)}) all-reduce(f32[256]{0:T(256)S(1)} %get-tuple-element.4, f32[256]{0:T(256)S(1)} %exponential_multiply_fusion), channel_id=1, replica_groups=mesh['dp'=8,'mp'=4] {'dp'}, use_global_device_ids=true, to_apply=%region_10.11 | all-reduce | flops 512 | bytes 4096 | tf_op jit(solution)/shard_map/psum | solution.py:154
  671.3 0.6 dynamic_slice.14
  671.8 0.1 convert_reduce_fusion
  672.0 6.0 all-reduce.7
  677.9 0.7 multiply_reduce_fusion.2
  678.6 1.3 fusion.33
  679.9 1.8 multiply_add_fusion
  (55 shorter events, 1.0 us)
Async XLA Ops:
  7.2 113.6 %copy-start = (bf16[4096,256]{1,0:T(8,128)(2,1)S(1)}, bf16[4096,256]{1,0:T(8,128)(2,1)}, u32[]{:S(2)}) copy-start(bf16[4096,256]{1,0:T(8,128)(2,1)} %param.22) | copy-start | bytes 6291460
  7.2 78.5 %all-gather.6.cloned.1.call-start = ((), (), s32[]{:S(2)}) async-start(), calls=%async_computation.1 | async-start | bytes 4718592 | tf_op jit(solution)/shard_map/all_gather | solution.py:62
  7.9 100.7 %all-gather.8.cloned.1.call-start = ((), (), s32[]{:S(2)}) async-start(), calls=%async_computation.2 | async-start | bytes 1310720 | tf_op jit(solution)/shard_map/all_gather | solution.py:81
  93.3 58.5 %reduce-scatter.2.cloned.1.call-start = ((), (), s32[]{:S(2)}) async-start(), calls=%async_computation.3 | async-start | bytes 1310720 | tf_op jit(solution)/shard_map/reduce_scatter | solution.py:114
  97.5 12.8 %copy-start.3 = (f32[4096]{0:T(1024)S(1)}, f32[4096]{0:T(1024)}, u32[]{:S(2)}) copy-start(f32[4096]{0:T(1024)} %param.19) | copy-start | bytes 49156
  110.2 3.0 copy-start.2
  118.2 2.6 copy-start.4
  119.5 1.4 copy-start.1
  120.8 0.7 copy-start.11
  122.9 30.2 %copy-start.5 = (f32[4096]{0:T(1024)S(1)}, f32[4096]{0:T(1024)}, u32[]{:S(2)}) copy-start(f32[4096]{0:T(1024)} %param.24) | copy-start | bytes 49156
  126.8 77.6 %all-gather.10.cloned.1.call-start = ((), (), s32[]{:S(2)}) async-start(), calls=%async_computation.4 | async-start | bytes 2359296 | tf_op jit(solution)/shard_map/all_gather | solution.py:131
  155.1 1.3 copy-start.10
  155.1 1.4 copy-start.6
  155.1 442.0 %all-gather.12.cloned.1.call-start = ((), (), s32[]{:S(2)}) async-start(), calls=%async_computation.5 | async-start | bytes 83886080 | tf_op jit(solution)/shard_map/all_gather | solution.py:141
  649.0 28.9 %copy-start.8 = (f32[22]{0:T(128)S(1)}, f32[22]{0:T(128)}, u32[]{:S(2)}) copy-start(f32[22]{0:T(128)} %param.26) | copy-start | bytes 268
  649.0 28.9 %copy-start.9 = (f32[22]{0:T(128)S(1)}, f32[22]{0:T(128)}, u32[]{:S(2)}) copy-start(f32[22]{0:T(128)} %param.27) | copy-start | bytes 268
  678.6 3.1 copy-start.7
Sparse Core Ops, SparseCore 0:
  10.1 75.5 all-gather.5
  93.4 15.2 all-gather.7
  127.0 24.7 reduce-scatter.1
  155.2 49.1 all-gather.9
  205.8 391.2 all-gather.11
where the time goes:
time: 689 us; the launch traced here: 688 us
  waiting for transfers between devices  493 us (72%)
  blocking collectives  94.2 us (14%)
  matrix products  51.6 us (7%)
  local copies, waits for them, and re-layouts  18.6 us (3%)
  between operations  15.3 us (2%)
  other arithmetic  15.2 us (2%)
    all_gather x1, waiting for transfers between devices, local(): lax.all_gather(w_vocab, 'mp', axis=0, tiled=True)  393 us
    all_gather x1, waiting for transfers between devices, local(): lax.all_gather(embedded, 'dp', axis=0, tiled=True)  58.5 us
    dot_general x1, matrix products, local(): jnp.dot(all_rows, lax.all_gather(w_vocab, 'mp', axis=0, tiled=True), pref...  30.6 us
    all_gather x1, blocking collectives, local(): lax.all_gather(targets, 'dp', axis=0, tiled=True)  26.2 us
    reduce_scatter x1, waiting for transfers between devices, local(): lax.psum_scatter(jnp.dot(mixed_heads, w_out, preferred_element_type=jnp.f...  24.9 us
    unnamed x2, blocking collectives  23.6 us
    pmax x1, blocking collectives, local(): top_all = lax.pmax(row_top, 'dp')  21.3 us
    psum x1, blocking collectives, local(): summed = lax.psum((spread * jnp.exp(row_top - top_all), picked), 'dp')  17.1 us
  transfers between devices with their start and end apart: 5, of which 5 were waited for; matrix products, arithmetic and copies ran while one was open for 2% of the time, Pallas kernels for 0%

commit v1 on v0

--- a/solution.py
+++ b/solution.py
@@ -138,7 +138,9 @@
     vocab_local = w_vocab.shape[1]
     logits = jnp.dot(
         all_rows,
-        lax.all_gather(w_vocab, "mp", axis=0, tiled=True),
+        jnp.concatenate(
+            lax.all_to_all(jnp.stack([w_vocab] * lax.axis_size("mp")), "mp", 0, 0), axis=0
+        ),
         preferred_element_type=jnp.float32,
     )
     row_top = jnp.max(logits, axis=1)

time: 689 us -> 874 us (1.27)
  waiting for transfers between devices: 493 us -> 644 us
  local copies, waits for them, and re-layouts: 18.6 us -> 43.5 us
  starting transfers between devices: 0.2 us -> 13.5 us
    all_to_all x0 -> x1, waiting for transfers between devices: none -> 528 us  [local(): lax.all_to_all(jnp.stack([w_vocab] * lax.axis_size('mp')), 'mp', 0, 0)]
    all_gather x1 -> x0, waiting for transfers between devices: 393 us -> none  [local(): lax.all_gather(w_vocab, 'mp', axis=0, tiled=True)]
    another operation x0 -> x1, local copies, waits for them, and re-layouts: none -> 26.9 us  [local(): jnp.stack([w_vocab] * lax.axis_size('mp'))]
    all_to_all x0 -> x1, starting transfers between devices: none -> 13.1 us  [local(): lax.all_to_all(jnp.stack([w_vocab] * lax.axis_size('mp')), 'mp', 0, 0)]
  transfers between devices with their start and end apart: 5 -> 5, of which waited for: 5 -> 5; matrix products, arithmetic and copies ran while one was open for 2% -> 4% of each run, Pallas kernels for 0% -> 0%
where the time goes in v1:
time: 874 us
  waiting for transfers between devices  644 us (74%)
  blocking collectives  94.8 us (11%)
  matrix products  46.9 us (5%)
  local copies, waits for them, and re-layouts  43.5 us (5%)
  other arithmetic  15.9 us (2%)
  between operations  15.3 us (2%)
  starting transfers between devices  13.5 us (2%)
    all_to_all x1, waiting for transfers between devices, local(): lax.all_to_all(jnp.stack([w_vocab] * lax.axis_size('mp')), 'mp', 0, 0)  528 us
    all_gather x1, waiting for transfers between devices, local(): lax.all_gather(embedded, 'dp', axis=0, tiled=True)  62.4 us
    reduce_scatter x1, waiting for transfers between devices, local(): lax.psum_scatter(jnp.dot(mixed_heads, w_out, preferred_element_type=jnp.f...  30.6 us
    dot_general x1, matrix products, local(): jnp.dot(all_rows, jnp.concatenate(lax.all_to_all(jnp.stack([w_vocab] * la...  30.6 us
    another operation x1, local copies, waits for them, and re-layouts, local(): jnp.stack([w_vocab] * lax.axis_size('mp'))  26.9 us
    all_gather x1, blocking collectives, local(): lax.all_gather(targets, 'dp', axis=0, tiled=True)  26.2 us
    unnamed x2, blocking collectives  23.3 us
    pmax x1, blocking collectives, local(): top_all = lax.pmax(row_top, 'dp')  22.5 us
  transfers between devices with their start and end apart: 5, of which 5 were waited for; matrix products, arithmetic and copies ran while one was open for 4% of the time, Pallas kernels for 0%

profile of v1, /device:TPU:0, one launch (start us, length us, event | category | flops | bytes accessed | tf_op | source)
XLA Modules:
  0.0 873.5 jit_solution(14914921144197956774)
XLA Ops:
  7.2 26.9 %stack.2 = bf16[4,1024,8192]{2,1,0:T(8,128)(2,1)} broadcast(bf16[1024,8192]{1,0:T(8,128)(2,1)} %param.25), dimensions={1,2} | broadcast | bytes 83886080 | tf_op jit(solution)/shard_map/stack | solution.py:142
  34.1 13.1 %all-to-all-start = ((bf16[4,1024,8192]{2,1,0:T(8,128)(2,1)}), bf16[4,1024,8192]{2,1,0:T(8,128)(2,1)}, u32[]{:S(2)}, u32[]{:S(2)}) async-start(bf16[4,1024,8192]{2,1,0:T(8,128)(2,1)} %stack.2), calls=%async_computation.1 | async-start | bytes 134217728 | tf_op jit(solution)/shard_map/all_to_all | solution.py:142
  47.3 0.7 all-gather.5.cloned.1.call-update
  48.1 0.6 dynamic-slice
  49.3 0.2 dynamic-update-slice
  49.6 0.2 dynamic-update-slice.2
  49.8 0.7 gather_fusion
  50.5 13.1 %all-reduce.5 = (s32[32]{0:T(128)S(1)}, s32[32]{0:T(128)S(1)}) all-reduce(s32[32]{0:T(128)S(1)} %dynamic-update-slice, s32[32]{0:T(128)S(1)} %dynamic-update-slice.2), channel_id=1, replica_groups=mesh['dp'=8,'mp'=4] {'dp'}, use_global_device_ids=true, to_apply=%add | all-reduce | flops 64 | bytes 512
  63.6 0.2 select_reduce_fusion.2
  63.8 62.4 %all-gather.5.cloned.1.call-done = bf16[32,64,1024]{2,1,0:T(8,128)(2,1)} async-done(((bf16[4,64,1024]{2,1,0:T(8,128)(2,1)}), bf16[32,64,1024]{2,1,0:T(8,128)(2,1)}) %all-gather.5.cloned.1.call-update) | async-done | bytes 4194320 | tf_op jit(solution)/shard_map/all_gather | solution.py:62
  126.2 6.8 fusion.1
  133.0 0.7 copy.77
  133.8 0.2 reduce-scatter.2.cloned.1.call-start
  134.0 4.1 copy.67
  138.1 6.4 copy.66
  144.6 0.1 fusion.21
  144.8 10.1 %all-gather.7.cloned.1.call-done = bf16[2,64,4096]{2,1,0:T(8,128)(2,1)} async-done(((bf16[2,64,1024]{2,1,0:T(8,128)(2,1)}), bf16[2,64,4096]{2,1,0:T(8,128)(2,1)}) %all-gather.7.cloned.1.call-update) | async-done | bytes 1048592 | tf_op jit(solution)/shard_map/all_gather | solution.py:81
  154.9 1.5 multiply_reduce_fusion
  156.5 1.4 bitcast_convert_fusion
  157.9 1.3 copy-done.2
  159.2 0.5 convolution_convert_fusion.2
  159.8 0.7 copy-done.3
  160.5 2.6 fusion.10
  163.3 1.5 fusion.12
  164.8 0.2 subtract_convert_fusion
  165.0 0.3 fusion.34
  165.4 0.3 fusion.4
  165.7 0.3 fusion.6
  166.1 3.9 convolution_convert_fusion
  170.0 30.6 %reduce-scatter.2.cloned.1.call-done = bf16[32,4096]{1,0:T(8,128)(2,1)} async-done(((bf16[128,4096]{1,0:T(8,128)(2,1)}), bf16[32,4096]{1,0:T(8,128)(2,1)}) %reduce-scatter.2.cloned.1.call-update) | async-done | bytes 262160 | tf_op jit(solution)/shard_map/reduce_scatter | solution.py:114
  200.7 1.3 multiply_reduce_fusion.1
  202.0 2.0 multiply_convert_fusion.3
  204.8 26.2 %all-gather = s32[8,4,64]{2,1,0:T(4,128)S(1)} all-gather(s32[1,4,64]{2,1,0:T(4,128)S(1)} %bitcast.57), channel_id=1, replica_groups=mesh['dp'=8,'mp'=4] {'dp'}, dimensions={0}, use_global_device_ids=true | all-gather | bytes 9216 | tf_op jit(solution)/shard_map/all_gather | solution.py:63
  230.9 0.1 fusion.38
  231.2 0.2 dynamic-slice_dynamic-update-slice_fusion
  231.3 0.2 dynamic-slice_dynamic-update-slice_fusion.1
  231.5 10.2 %all-reduce.4 = (s32[256]{0:T(256)S(1)}, s32[256]{0:T(256)S(1)}) all-reduce(s32[256]{0:T(256)S(1)} %dynamic-slice_dynamic-update-slice_fusion.1, s32[256]{0:T(256)S(1)} %dynamic-slice_dynamic-update-slice_fusion), channel_id=1, replica_groups=mesh['dp'=8,'mp'=4] {'dp'}, use_global_device_ids=true, to_apply=%add.1 | all-reduce | flops 512 | bytes 4096
  241.6 12.0 %all-gather.9.cloned.1.call-done = bf16[256,4096]{1,0:T(8,128)(2,1)} async-done(((bf16[32,4096]{1,0:T(8,128)(2,1)}), bf16[256,4096]{1,0:T(8,128)(2,1)}) %all-gather.9.cloned.1.call-update) | async-done | bytes 2097168 | tf_op jit(solution)/shard_map/all_gather | solution.py:131
  253.6 527.9 %all-to-all-done = bf16[4,1024,8192]{2,1,0:T(8,128)(2,1)} async-done(((bf16[4,1024,8192]{2,1,0:T(8,128)(2,1)}), bf16[4,1024,8192]{2,1,0:T(8,128)(2,1)}, u32[]{:S(2)}, u32[]{:S(2)}) %all-to-all-start) | async-done | bytes 67108896 | tf_op jit(solution)/shard_map/all_to_all | solution.py:142
  781.5 30.6 %fusion.37 = (f32[256]{0:T(256)S(1)}, f32[256,8192]{1,0:T(8,128)}) fusion(bf16[256,4096]{1,0:T(8,128)(2,1)} %all-gather.9.cloned.1.call-done, bf16[4096,8192]{1,0:T(8,128)(2,1)} %bitcast.16), kind=kOutput, calls=%fused_computation.79 | convolution fusion | flops 17181966336 | bytes 77595648 | tf_op jit(solution)/shard_map/dot_general | solution.py:139
  812.1 22.5 %pmax.7 = f32[256]{0:T(256)S(1)} all-reduce(f32[256]{0:T(256)S(1)} %get-tuple-element.25), channel_id=1, replica_groups=mesh['dp'=8,'mp'=4] {'dp'}, use_global_device_ids=true, to_apply=%region_6.7 | all-reduce | flops 256 | bytes 2048 | tf_op jit(solution)/shard_map/pmax | solution.py:155
  834.5 5.1 exponential_reduce_fusion
  839.6 17.1 %all-reduce.6 = (f32[256]{0:T(256)S(1)}, f32[256]{0:T(256)S(1)}) all-reduce(f32[256]{0:T(256)S(1)} %get-tuple-element.4, f32[256]{0:T(256)S(1)} %exponential_multiply_fusion), channel_id=1, replica_groups=mesh['dp'=8,'mp'=4] {'dp'}, use_global_device_ids=true, to_apply=%region_10.11 | all-reduce | flops 512 | bytes 4096 | tf_op jit(solution)/shard_map/psum | solution.py:156
  856.8 0.6 dynamic_slice.14
  857.5 5.8 all-reduce.7
  863.2 0.7 multiply_reduce_fusion.2
  863.9 1.3 fusion.33
  865.2 1.8 multiply_add_fusion
  (59 shorter events, 1.2 us)
Async XLA Ops:
  7.2 152.1 %copy-start = (bf16[4096,256]{1,0:T(8,128)(2,1)S(1)}, bf16[4096,256]{1,0:T(8,128)(2,1)}, u32[]{:S(2)}) copy-start(bf16[4096,256]{1,0:T(8,128)(2,1)} %param.22) | copy-start | bytes 6291460
  34.1 14.0 %copy-start.13 = (u32[32]{0:T(128)S(1)}, u32[32]{0:T(128)}, u32[]{:S(2)}) copy-start(u32[32]{0:T(128)} %constant.94) | copy-start | bytes 388
  34.1 15.2 %copy-start.11 = (s32[4]{0:T(128)S(1)}, s32[4]{0:T(128)}, u32[]{:S(2)}) copy-start(s32[4]{0:T(128)} %param.18) | copy-start | bytes 52
  34.1 15.5 %copy-start.12 = (s32[4]{0:T(128)S(1)}, s32[4]{0:T(128)}, u32[]{:S(2)}) copy-start(s32[4]{0:T(128)} %param.16) | copy-start | bytes 52
  34.1 15.7 %copy-start.1 = (s32[8]{0:T(128)S(1)}, s32[8]{0:T(128)}, u32[]{:S(2)}) copy-start(s32[8]{0:T(128)} %param.17) | copy-start | bytes 100
  34.1 747.3 %all-to-all-start = ((bf16[4,1024,8192]{2,1,0:T(8,128)(2,1)}), bf16[4,1024,8192]{2,1,0:T(8,128)(2,1)}, u32[]{:S(2)}, u32[]{:S(2)}) async-start(bf16[4,1024,8192]{2,1,0:T(8,128)(2,1)} %stack.2), calls=%async_computation.1 | async-start | bytes 134217728 | tf_op jit(solution)/shard_map/all_to_all | solution.py:142
  47.3 79.0 %all-gather.5.cloned.1.call-start = ((), (), s32[]{:S(2)}) async-start(), calls=%async_computation.2 | async-start | bytes 4718592 | tf_op jit(solution)/shard_map/all_gather | solution.py:62
  48.0 106.9 %all-gather.7.cloned.1.call-start = ((), (), s32[]{:S(2)}) async-start(), calls=%async_computation.3 | async-start | bytes 1310720 | tf_op jit(solution)/shard_map/all_gather | solution.py:81
  133.8 66.9 %reduce-scatter.2.cloned.1.call-start = ((), (), s32[]{:S(2)}) async-start(), calls=%async_computation.4 | async-start | bytes 1310720 | tf_op jit(solution)/shard_map/reduce_scatter | solution.py:114
  144.8 14.5 %copy-start.5 = (f32[4096]{0:T(1024)S(1)}, f32[4096]{0:T(1024)}, u32[]{:S(2)}) copy-start(f32[4096]{0:T(1024)} %param.19) | copy-start | bytes 49156
  157.9 1.3 copy-start.2
  159.2 1.2 copy-start.3
  160.5 2.8 copy-start.4
  166.0 35.9 %copy-start.6 = (f32[4096]{0:T(1024)S(1)}, f32[4096]{0:T(1024)}, u32[]{:S(2)}) copy-start(f32[4096]{0:T(1024)} %param.24) | copy-start | bytes 49156
  170.0 34.8 %copy-start.7 = (s32[4,64]{1,0:T(4,128)S(1)}, s32[4,64]{1,0:T(4,128)}, u32[]{:S(2)}) copy-start(s32[4,64]{1,0:T(4,128)} %param.15) | copy-start | bytes 3076
  170.0 83.6 %all-gather.9.cloned.1.call-start = ((), (), s32[]{:S(2)}) async-start(), calls=%async_computation.5 | async-start | bytes 2359296 | tf_op jit(solution)/shard_map/all_gather | solution.py:131
  834.5 28.7 %copy-start.9 = (f32[22]{0:T(128)S(1)}, f32[22]{0:T(128)}, u32[]{:S(2)}) copy-start(f32[22]{0:T(128)} %param.26) | copy-start | bytes 268
  834.5 28.7 %copy-start.10 = (f32[22]{0:T(128)S(1)}, f32[22]{0:T(128)}, u32[]{:S(2)}) copy-start(f32[22]{0:T(128)} %param.27) | copy-start | bytes 268
  863.9 3.1 copy-start.8
Sparse Core Ops, SparseCore 0:
  50.2 75.9 all-gather.4
  133.9 20.9 all-gather.6
  170.1 30.4 reduce-scatter.1
  204.1 49.4 all-gather.8
